TPU v7x, 32 devices: a whole 2x2x4 slice. The times are simulated.
32 devices in a mesh: layer: 2 (over y), feat: 4 (over x, core), width: 4 (over z).
Axes of the slice: x: 2, y: 2, z: 4, core: 2. Of those that a mesh axis runs over, the one named last changes fastest.
Arguments:
- resid: bfloat16 [2, 128, 2048], P(None, 'layer', 'width'), may hold values from -6 to 6
- enc_w: bfloat16 [2, 2048, 65536], P(None, 'width', ('layer', 'feat')), may hold values from -0.125 to 0.125
- enc_b: float32 [2, 65536], P(None, ('layer', 'feat')), may hold values from -3 to 3
- dec_w: float32 [3, 65536, 2048], P(None, ('layer', 'feat'), 'width'), may hold values from -0.03125 to 0.03125
- dec_b: float32 [2, 2048], P(None, 'width'), may hold values from -2 to 2
- target: float32 [2, 128, 2048], P(None, ('layer', 'feat'), 'width'), may hold values from -6 to 6
Outputs:
- recon: float32 [2, 128, 2048], P(None, ('layer', 'feat'), 'width')
- err: float32 [2, 128], P(None, ('layer', 'feat'))
All inputs are finite; a program needn't handle non-finite values.
Results may differ from a plain program's by a relative error of at most 0.00035.
Values may be sent and summed in bfloat16 or wider, within the bound.
No kernel may reach another device: no remote copies, remote signals or barrier semaphores. Data moves between devices by JAX's collectives and lax.ppermute only.
A program may use at most 128 MiB of HBM per device.

v0:
```python
import jax
import jax.numpy as jnp
from jax import lax
from jax.sharding import PartitionSpec as P


def decode_rows(act, dec_w, target_idx):
    total = None
    for layer_idx in range(target_idx + 1):
        block = target_idx * (target_idx + 1) // 2 + layer_idx
        rows = act[layer_idx]
        term = jnp.dot(
            rows, dec_w[block], precision=lax.Precision.HIGHEST, preferred_element_type=jnp.float32
        )
        total = term if total is None else total + term
    return total


def per_device(resid, enc_w, enc_b, dec_w, dec_b, target):
    layers = resid.shape[0]
    gathered = lax.all_gather(resid, "layer", axis=1, tiled=True)
    tokens = gathered.shape[1]
    partial_pre = jnp.einsum("ltd,ldf->ltf", gathered, enc_w, preferred_element_type=jnp.float32)
    pre = lax.psum(partial_pre, "width")
    act = jnp.maximum(pre + enc_b[:, None, :], 0.0)
    own_rows = tokens // lax.axis_size(("layer", "feat"))
    summed = lax.psum_scatter(
        jnp.concatenate(
            [decode_rows(act, dec_w, target_idx) for target_idx in range(layers)], axis=1
        ),
        ("layer", "feat"),
        scatter_dimension=0,
        tiled=True,
    )
    summed = summed.reshape(own_rows, layers, dec_w.shape[2]).transpose(1, 0, 2)
    recon = summed + dec_b[:, None, :]
    diff = recon - target
    sq_error, sq_target = lax.psum(
        (jnp.sum(diff * diff, axis=2), jnp.sum(target * target, axis=2)), "width"
    )
    err = sq_error / (sq_target + 1e-06)
    return (recon, err)


def solution(mesh):
    in_specs = (
        P(None, "layer", "width"),
        P(None, "width", ("layer", "feat")),
        P(None, ("layer", "feat")),
        P(None, ("layer", "feat"), "width"),
        P(None, "width"),
        P(None, ("layer", "feat"), "width"),
    )
    out_specs = (P(None, ("layer", "feat"), "width"), P(None, ("layer", "feat")))
    return jax.shard_map(
        per_device, mesh=mesh, in_specs=in_specs, out_specs=out_specs, check_vma=False
    )
```

profile of v0, /device:TPU:0, one launch (start us, length us, event | category | flops | bytes accessed | tf_op | source)
XLA Modules:
  0.0 413.2 jit_solution(15221711624656479680)
XLA Ops:
  7.2 0.0 all-reduce.3.cloned.1.call-start
  7.2 7.4 %all_gather.3 = bf16[2,128,512]{2,1,0:T(8,128)(2,1)S(1)} all-gather(bf16[2,64,512]{2,1,0:T(8,128)(2,1)} %param.6), channel_id=1, replica_groups=mesh['layer'=2,'feat'=4,'width'=4] {'layer'}, dimensions={1}, use_global_device_ids=true | all-gather | bytes 393216 | tf_op jit(solution)/shard_map/all_gather | solution.py:21
  14.6 11.3 %fusion.14 = f32[2,128,8192]{2,1,0:T(8,128)} fusion(bf16[2,128,512]{2,1,0:T(8,128)(2,1)S(1)} %all_gather.3, bf16[2,512,8192]{2,1,0:T(8,128)(2,1)} %param.7), kind=kOutput, calls=%fused_computation.19 | convolution fusion | flops 2147483648 | bytes 25427968 | tf_op jit(solution)/shard_map/ltd,ldf->ltf/dot_general | solution.py:23
  26.0 0.0 copy-start
  26.0 0.0 all-reduce.3.cloned.1.call-update
  26.0 0.0 reduce-scatter.2.cloned.1.call-start
  26.0 292.4 %all-reduce.3.cloned.1.call-done = f32[2,128,8192]{2,1,0:T(8,128)} async-done(((f32[2,128,8192]{2,1,0:T(8,128)}), f32[2,128,8192]{2,1,0:T(8,128)}) %all-reduce.3.cloned.1.call-update) | async-done | bytes 8388624 | tf_op jit(solution)/shard_map/psum | solution.py:24
  318.4 0.0 copy-done
  318.4 4.2 %add_maximum_fusion = f32[2,128,8192]{2,1,0:T(8,128)S(1)} fusion(f32[2,128,8192]{2,1,0:T(8,128)} %all-reduce.3.cloned.1.call-done, f32[2,8192]{1,0:T(2,128)S(1)} %copy-done), kind=kLoop, calls=%fused_computation.9 | loop fusion | flops 4194304 | bytes 16842752 | tf_op jit(solution)/shard_map/max | solution.py:25
  322.6 11.9 %fusion = f32[128,512]{1,0:T(8,128)S(1)} fusion(f32[3,8192,512]{2,1,0:T(8,128)} %param.9, f32[2,128,8192]{2,1,0:T(8,128)S(1)} %add_maximum_fusion), kind=kOutput, calls=%fused_computation | convolution fusion | flops 6442450944 | bytes 21233664 | tf_op jit(solution)/shard_map/dot_general | solution.py:12
  334.5 11.9 %fusion.4 = f32[128,512]{1,0:T(8,128)S(1)} fusion(f32[3,8192,512]{2,1,0:T(8,128)} %param.9, f32[2,128,8192]{2,1,0:T(8,128)S(1)} %add_maximum_fusion), kind=kOutput, calls=%fused_computation.4 | convolution fusion | flops 6442450944 | bytes 21233664 | tf_op jit(solution)/shard_map/dot_general | solution.py:12
  346.4 0.0 copy-start.1
  346.4 0.0 copy-start.2
  346.4 12.1 %fusion.9 = f32[128,512]{1,0:T(8,128)S(1)} fusion(f32[128,512]{1,0:T(8,128)S(1)} %fusion, f32[3,8192,512]{2,1,0:T(8,128)} %param.9, f32[2,128,8192]{2,1,0:T(8,128)S(1)} %add_maximum_fusion), kind=kOutput, calls=%fused_computation.12 | convolution fusion | flops 6442516480 | bytes 21495808 | tf_op jit(solution)/shard_map/dot_general | solution.py:12
  358.5 0.8 pad_maximum_fusion
  359.3 0.0 reduce-scatter.2.cloned.1.call-update
  359.4 33.2 %reduce-scatter.2.cloned.1.call-done = f32[16,1024]{1,0:T(8,128)} async-done(((f32[128,1024]{1,0:T(8,128)}), f32[16,1024]{1,0:T(8,128)}) %reduce-scatter.2.cloned.1.call-update) | async-done | bytes 65552 | tf_op jit(solution)/shard_map/reduce_scatter | solution.py:27
  392.6 0.0 copy-done.1
  392.6 0.0 copy-done.2
  392.6 1.5 multiply_reduce_fusion
  394.1 11.6 %all-reduce = (f32[2,16]{1,0:T(2,128)S(1)}, f32[2,16]{1,0:T(2,128)S(1)}) all-reduce(f32[2,16]{1,0:T(2,128)S(1)} %get-tuple-element.3, f32[2,16]{1,0:T(2,128)S(1)} %get-tuple-element.2), channel_id=1, replica_groups=mesh['layer'=2,'feat'=4,'width'=4] {'width'}, use_global_device_ids=true, to_apply=%region_3.0 | all-reduce | flops 64 | bytes 512 | tf_op jit(solution)/shard_map/psum | solution.py:38
  405.8 0.6 add_divide_fusion
Async XLA Ops:
  7.2 311.2 %all-reduce.3.cloned.1.call-start = ((), (), s32[]{:S(2)}) async-start(), calls=%async_computation.1 | async-start | bytes 16777216 | tf_op jit(solution)/shard_map/psum | solution.py:24
  26.0 292.4 %copy-start = (f32[2,8192]{1,0:T(2,128)S(1)}, f32[2,8192]{1,0:T(2,128)}, u32[]{:S(2)}) copy-start(f32[2,8192]{1,0:T(2,128)} %param.8) | copy-start | bytes 196612
  26.0 366.6 %reduce-scatter.2.cloned.1.call-start = ((), (), s32[]{:S(2)}) async-start(), calls=%async_computation.2 | async-start | bytes 589824 | tf_op jit(solution)/shard_map/reduce_scatter | solution.py:27
  346.4 46.2 %copy-start.1 = (f32[2,16,512]{2,1,0:T(8,128)S(1)}, f32[2,16,512]{2,1,0:T(8,128)}, u32[]{:S(2)}) copy-start(f32[2,16,512]{2,1,0:T(8,128)} %param.11) | copy-start | bytes 196612
  346.4 46.2 %copy-start.2 = (f32[2,512]{1,0:T(2,128)S(1)}, f32[2,512]{1,0:T(2,128)}, u32[]{:S(2)}) copy-start(f32[2,512]{1,0:T(2,128)} %param.10) | copy-start | bytes 12292
Sparse Core Ops, SparseCore 0:
  26.1 292.2 all-reduce.2
  359.5 33.0 reduce-scatter.1
where the time goes:
time: 413 us
  waiting for transfers between devices  326 us (79%)
  matrix products  47.2 us (11%)
  blocking collectives  19.1 us (5%)
  between operations  14.1 us (3%)
  other arithmetic  7.07 us (2%)
    psum x1, waiting for transfers between devices, per_device(): pre = lax.psum(partial_pre, 'width')  292 us
    dot_general x3, matrix products, decode_rows(): jnp.dot(rows, dec_w[block], precision=lax.Precision.HIGHEST, preferred_el...  35.9 us
    reduce_scatter x1, waiting for transfers between devices, per_device(): lax.psum_scatter(jnp.concatenate([decode_rows(act, dec_w, target_idx) for...  33.2 us
    psum x1, blocking collectives, per_device(): lax.psum((jnp.sum(diff * diff, axis=2), jnp.sum(target * target, axis=2))...  11.6 us
    dot_general x1, matrix products, per_device(): jnp.einsum('ltd,ldf->ltf', gathered, enc_w, preferred_element_type=jnp.fl...  11.3 us
  transfers between devices with their start and end apart: 2, of which 2 were waited for; matrix products, arithmetic and copies ran while one was open for 0% of the time, Pallas kernels for 0%

commit v1 on v0

--- a/solution.py
+++ b/solution.py
@@ -17,11 +17,23 @@
 
 
 def per_device(resid, enc_w, enc_b, dec_w, dec_b, target):
+
+    def stages_all_make(local):
+        axis_id = "width"
+        size_here = lax.axis_size(axis_id)
+        local_next = lambda w1: [(ix, ix ^ w1) for ix in range(size_here)]
+        block_next = local
+        for to_i in range(size_here.bit_length() - 1):
+            t1 = local_next(1 << to_i)
+            block_now = lax.ppermute(block_next, axis_id, t1)
+            block_next = block_next + block_now
+        return block_next
+
     layers = resid.shape[0]
     gathered = lax.all_gather(resid, "layer", axis=1, tiled=True)
     tokens = gathered.shape[1]
     partial_pre = jnp.einsum("ltd,ldf->ltf", gathered, enc_w, preferred_element_type=jnp.float32)
-    pre = lax.psum(partial_pre, "width")
+    pre = stages_all_make(partial_pre)
     act = jnp.maximum(pre + enc_b[:, None, :], 0.0)
     own_rows = tokens // lax.axis_size(("layer", "feat"))
     summed = lax.psum_scatter(

time: 413 us -> 684 us (1.66)
  waiting for transfers between devices: 326 us -> 574 us
  other arithmetic: 7.07 us -> 24.2 us
    ppermute x0 -> x2, waiting for transfers between devices: none -> 539 us  [stages_all_make(): block_now = lax.ppermute(block_next, axis_id, t1)]
    psum x1 -> x0, waiting for transfers between devices: 292 us -> none  [per_device(): pre = lax.psum(partial_pre, 'width')]
    add x0 -> x1, other arithmetic: none -> 10.3 us  [stages_all_make(): block_next = block_next + block_now]
    max x1, other arithmetic: 4.19 us -> 11.1 us  [per_device(): act = jnp.maximum(pre + enc_b[:, None, :], 0.0)]
  transfers between devices with their start and end apart: 2 -> 3, of which waited for: 2 -> 3; matrix products, arithmetic and copies ran while one was open for 0% -> 0% of each run, Pallas kernels for 0% -> 0%
where the time goes in v1:
time: 684 us
  waiting for transfers between devices  574 us (84%)
  matrix products  45.1 us (7%)
  other arithmetic  24.2 us (4%)
  blocking collectives  19.1 us (3%)
  between operations  14.1 us (2%)
    ppermute x2, waiting for transfers between devices, stages_all_make(): block_now = lax.ppermute(block_next, axis_id, t1)  539 us
    dot_general x3, matrix products, decode_rows(): jnp.dot(rows, dec_w[block], precision=lax.Precision.HIGHEST, preferred_el...  36.9 us
    reduce_scatter x1, waiting for transfers between devices, per_device(): lax.psum_scatter(jnp.concatenate([decode_rows(act, dec_w, target_idx) for...  35 us
  transfers between devices with their start and end apart: 3, of which 3 were waited for; matrix products, arithmetic and copies ran while one was open for 0% of the time, Pallas kernels for 0%

profile of v1, /device:TPU:0, one launch (start us, length us, event | category | flops | bytes accessed | tf_op | source)
XLA Modules:
  0.0 684.2 jit_solution(14321457187715697947)
XLA Ops:
  7.2 0.0 reduce-scatter.2.cloned.1.call-start
  7.2 7.4 %all_gather.3 = bf16[2,128,512]{2,1,0:T(8,128)(2,1)S(1)} all-gather(bf16[2,64,512]{2,1,0:T(8,128)(2,1)} %param.6), channel_id=1, replica_groups=mesh['layer'=2,'feat'=4,'width'=4] {'layer'}, dimensions={1}, use_global_device_ids=true | all-gather | bytes 393216 | tf_op jit(solution)/shard_map/all_gather | solution.py:33
  14.6 8.1 %fusion.14 = f32[2,128,8192]{2,1,0:T(8,128)S(1)} fusion(bf16[2,128,512]{2,1,0:T(8,128)(2,1)S(1)} %all_gather.3, bf16[2,512,8192]{2,1,0:T(8,128)(2,1)} %param.7), kind=kOutput, calls=%fused_computation.19 | convolution fusion | flops 2147483648 | bytes 25427968 | tf_op jit(solution)/shard_map/ltd,ldf->ltf/dot_general | solution.py:35
  22.8 0.0 copy-start
  22.8 3.2 copy-done
  26.0 0.0 copy-start.2
  26.0 1.7 collective-permute-start
  27.7 180.0 %collective-permute-done = f32[2,128,8192]{2,1,0:T(8,128)} collective-permute-done((f32[2,128,8192]{2,1,0:T(8,128)S(1)}, f32[2,128,8192]{2,1,0:T(8,128)}, u32[]{:S(2)}, u32[]{:S(2)}) %collective-permute-start) | collective-permute-done | bytes 8388640 | tf_op jit(solution)/shard_map/ppermute | solution.py:28
  207.7 10.3 %add.40 = f32[2,128,8192]{2,1,0:T(8,128)} add(f32[2,128,8192]{2,1,0:T(8,128)} %copy-done, f32[2,128,8192]{2,1,0:T(8,128)} %collective-permute-done) | non-fusion elementwise | flops 2097152 | bytes 25165824 | tf_op jit(solution)/shard_map/add | solution.py:29
  218.0 2.5 collective-permute-start.1
  220.4 359.3 %collective-permute-done.1 = f32[2,128,8192]{2,1,0:T(8,128)} collective-permute-done((f32[2,128,8192]{2,1,0:T(8,128)}, f32[2,128,8192]{2,1,0:T(8,128)}, u32[]{:S(2)}, u32[]{:S(2)}) %collective-permute-start.1) | collective-permute-done | bytes 8388640 | tf_op jit(solution)/shard_map/ppermute | solution.py:28
  579.7 0.0 copy-done.2
  579.7 11.1 %add_maximum_fusion = f32[2,128,8192]{2,1,0:T(8,128)} fusion(f32[2,128,8192]{2,1,0:T(8,128)} %add.40, f32[2,128,8192]{2,1,0:T(8,128)} %collective-permute-done.1, f32[2,8192]{1,0:T(2,128)S(1)} %copy-done.2), kind=kLoop, calls=%fused_computation.9 | loop fusion | flops 6291456 | bytes 25231360 | tf_op jit(solution)/shard_map/max | solution.py:37
  590.8 0.0 copy-start.1
  590.8 12.9 %fusion = f32[128,512]{1,0:T(8,128)S(1)} fusion(f32[3,8192,512]{2,1,0:T(8,128)} %param.9, f32[2,128,8192]{2,1,0:T(8,128)} %add_maximum_fusion), kind=kOutput, calls=%fused_computation | convolution fusion | flops 6442450944 | bytes 21233664 | tf_op jit(solution)/shard_map/dot_general | solution.py:12
  603.7 0.0 copy-done.1
  603.8 11.9 %fusion.4 = f32[128,512]{1,0:T(8,128)S(1)} fusion(f32[3,8192,512]{2,1,0:T(8,128)} %param.9, f32[2,128,8192]{2,1,0:T(8,128)S(1)} %copy-done.1), kind=kOutput, calls=%fused_computation.4 | convolution fusion | flops 6442450944 | bytes 21233664 | tf_op jit(solution)/shard_map/dot_general | solution.py:12
  615.6 0.0 copy-start.3
  615.6 0.0 copy-start.4
  615.7 12.1 %fusion.9 = f32[128,512]{1,0:T(8,128)S(1)} fusion(f32[128,512]{1,0:T(8,128)S(1)} %fusion, f32[3,8192,512]{2,1,0:T(8,128)} %param.9, f32[2,128,8192]{2,1,0:T(8,128)S(1)} %copy-done.1), kind=kOutput, calls=%fused_computation.12 | convolution fusion | flops 6442516480 | bytes 21495808 | tf_op jit(solution)/shard_map/dot_general | solution.py:12
  627.8 0.8 pad_maximum_fusion
  628.6 0.0 reduce-scatter.2.cloned.1.call-update
  628.6 35.0 %reduce-scatter.2.cloned.1.call-done = f32[16,1024]{1,0:T(8,128)} async-done(((f32[128,1024]{1,0:T(8,128)}), f32[16,1024]{1,0:T(8,128)}) %reduce-scatter.2.cloned.1.call-update) | async-done | bytes 65552 | tf_op jit(solution)/shard_map/reduce_scatter | solution.py:39
  663.6 0.0 copy-done.3
  663.7 0.0 copy-done.4
  663.7 1.5 multiply_reduce_fusion
  665.1 11.6 %all-reduce = (f32[2,16]{1,0:T(2,128)S(1)}, f32[2,16]{1,0:T(2,128)S(1)}) all-reduce(f32[2,16]{1,0:T(2,128)S(1)} %get-tuple-element.3, f32[2,16]{1,0:T(2,128)S(1)} %get-tuple-element.2), channel_id=1, replica_groups=mesh['layer'=2,'feat'=4,'width'=4] {'width'}, use_global_device_ids=true, to_apply=%region_2.0 | all-reduce | flops 64 | bytes 512 | tf_op jit(solution)/shard_map/psum | solution.py:50
  676.8 0.6 add_divide_fusion
Async XLA Ops:
  7.2 656.5 %reduce-scatter.2.cloned.1.call-start = ((), (), s32[]{:S(2)}) async-start(), calls=%async_computation.1 | async-start | bytes 589824 | tf_op jit(solution)/shard_map/reduce_scatter | solution.py:39
  22.8 3.2 copy-start
  26.0 553.7 %copy-start.2 = (f32[2,8192]{1,0:T(2,128)S(1)}, f32[2,8192]{1,0:T(2,128)}, u32[]{:S(2)}) copy-start(f32[2,8192]{1,0:T(2,128)} %param.8) | copy-start | bytes 196612
  26.0 181.7 %collective-permute-start = (f32[2,128,8192]{2,1,0:T(8,128)S(1)}, f32[2,128,8192]{2,1,0:T(8,128)}, u32[]{:S(2)}, u32[]{:S(2)}) collective-permute-start(f32[2,128,8192]{2,1,0:T(8,128)S(1)} %fusion.14), channel_id=1, source_target_pairs={{0,1},{1,0},{2,3},{3,2},{4,5},{5,4},{6,7},{7,6},{8,9},{9,8},{10,11... | collective-permute-start | bytes 25165832 | tf_op jit(solution)/shard_map/ppermute | solution.py:28
  218.0 361.7 %collective-permute-start.1 = (f32[2,128,8192]{2,1,0:T(8,128)}, f32[2,128,8192]{2,1,0:T(8,128)}, u32[]{:S(2)}, u32[]{:S(2)}) collective-permute-start(f32[2,128,8192]{2,1,0:T(8,128)} %add.40), channel_id=1, source_target_pairs={{0,2},{1,3},{2,0},{3,1},{4,6},{5,7},{6,4},{7,5},{8,10},{9,11},{10,... | collective-permute-start | bytes 25165832 | tf_op jit(solution)/shard_map/ppermute | solution.py:28
  590.8 13.0 %copy-start.1 = (f32[2,128,8192]{2,1,0:T(8,128)S(1)}, f32[2,128,8192]{2,1,0:T(8,128)}, u32[]{:S(2)}) copy-start(f32[2,128,8192]{2,1,0:T(8,128)} %add_maximum_fusion) | copy-start | bytes 25165828
  615.6 48.0 %copy-start.3 = (f32[2,16,512]{2,1,0:T(8,128)S(1)}, f32[2,16,512]{2,1,0:T(8,128)}, u32[]{:S(2)}) copy-start(f32[2,16,512]{2,1,0:T(8,128)} %param.11) | copy-start | bytes 196612
  615.6 48.0 %copy-start.4 = (f32[2,512]{1,0:T(2,128)S(1)}, f32[2,512]{1,0:T(2,128)}, u32[]{:S(2)}) copy-start(f32[2,512]{1,0:T(2,128)} %param.10) | copy-start | bytes 12292
Sparse Core Ops, SparseCore 0:
  628.8 34.8 reduce-scatter.1
